TPU v7x, 512 devices: a whole 4x8x8 slice. The times are simulated.
512 devices in a mesh: section: 4 (over x), frame: 16 (over y_lo, z), chan: 8 (over y_hi, core).
Axes of the slice: x: 4, y: 8 (y_hi: 4, y_lo: 2; y = y_hi * 2 + y_lo), z: 8, core: 2. Of those that a mesh axis runs over, the one named last changes fastest.
Arguments:
- upstream: bfloat16 [512, 8, 16, 128], P('chan', None, 'frame'), may hold values from -6 to 6
- acts: bfloat16 [4, 512, 8, 16, 128], P('section', None, None, 'frame'), may hold values from -6 to 6
- weights: bfloat16 [4, 27, 512, 512], P('section', None, 'chan'), may hold values from -0.0625 to 0.0625
Outputs:
- grads: bfloat16 [4, 512, 8, 16, 128], P('section', 'chan', None, 'frame')
- weight_grads: bfloat16 [4, 27, 512, 512], P('section', None, 'chan')
All inputs are finite; a program needn't handle non-finite values.
Results may differ from a plain program's by a relative error of at most 0.03.
Values may be sent and summed in bfloat16 or wider, within the bound.
A program may use at most 64 MiB of HBM per device.

v0:
```python
import jax
import jax.numpy as jnp
from jax import lax
from jax.sharding import PartitionSpec as P

BLOCK_FRAMES = 2


def with_halo(cells, sides, width):
    for axis, dim in sides:
        count = lax.axis_size(axis)
        ends = count - 1
        head = lax.slice_in_dim(cells, 0, width, axis=dim)
        tail = lax.slice_in_dim(cells, cells.shape[dim] - width, cells.shape[dim], axis=dim)
        cells = jnp.concatenate(
            [
                lax.ppermute(tail, axis, [(i, (i + 1) % count) for i in range(ends)]),
                cells,
                lax.ppermute(head, axis, [((i + 1) % count, i) for i in range(ends)]),
            ],
            axis=dim,
        )
    return cells


def shifted(value, axis, steps):
    count = lax.axis_size(axis)
    leading, last = (max(0, -steps), min(count, count - steps))
    return lax.ppermute(value, axis, [(source, source + steps) for source in range(leading, last)])


def derivative(stored):
    logistic = jax.nn.sigmoid(stored)
    return logistic * (1.0 + stored * (1.0 - logistic))


def tap_matrix(extended, frames_n, rows_n, width_n):
    pieces = []
    for t_lag in range(3):
        for r_off in (-1, 0, 1):
            for w_off in (-1, 0, 1):
                pieces.append(
                    extended[
                        :,
                        t_lag : t_lag + frames_n,
                        1 - r_off : 1 - r_off + rows_n,
                        1 - w_off : 1 - w_off + width_n,
                    ]
                )
    stacked = jnp.stack(pieces, axis=0)
    return stacked.reshape(stacked.shape[0] * stacked.shape[1], -1)


def body(upstream, acts, weights):
    group = upstream.shape[0]
    frames_all = upstream.shape[1]
    rows_n = upstream.shape[2]
    width_n = upstream.shape[3]
    channels = acts.shape[1]
    blocks_n = frames_all // BLOCK_FRAMES
    cells = BLOCK_FRAMES * rows_n * width_n
    sections = lax.axis_size("section")
    section_pos = lax.axis_index("section")
    chan_pos = lax.axis_index("chan")
    kernel_mat = weights[0].reshape(27 * group, channels)
    stored_all = acts[0]
    later = jnp.zeros((group, 2, rows_n + 2, width_n), jnp.bfloat16)
    inbound = jnp.zeros((group, BLOCK_FRAMES, rows_n, width_n), jnp.bfloat16)
    results = jnp.zeros((group, frames_all, rows_n, width_n), jnp.bfloat16)
    kernel_sum = jnp.zeros((27 * group, channels), jnp.float32)
    ticks = blocks_n + sections - 1
    for tick in range(ticks):
        order = tick - section_pos
        active = jnp.logical_and(order >= 0, order < blocks_n)
        first = (blocks_n - 1 - jnp.clip(order, 0, blocks_n - 1)) * BLOCK_FRAMES
        fresh = lax.dynamic_slice_in_dim(upstream, first, BLOCK_FRAMES, 1)
        current = jnp.where(section_pos == 0, fresh, inbound)
        framed = with_halo(current, (("frame", 2),), 1)
        extended = jnp.pad(
            jnp.concatenate([framed, later], axis=1), ((0, 0), (0, 0), (0, 0), (1, 1))
        )
        taps_mat = tap_matrix(extended, BLOCK_FRAMES, rows_n, width_n)
        stored = lax.dynamic_slice_in_dim(stored_all, first, BLOCK_FRAMES, 1)

        def busy(operand):
            return lax.dot_general(
                kernel_mat, taps_mat, (((0,), (0,)), ((), ())), preferred_element_type=jnp.float32
            )

        def resting(operand):
            return jnp.zeros((group * lax.axis_size("chan"), cells), jnp.float32)

        summed = lax.psum_scatter(
            lax.cond(active, busy, resting, 0).astype(jnp.bfloat16),
            "chan",
            scatter_dimension=0,
            tiled=True,
        ).astype(jnp.float32)
        own = lax.dynamic_slice_in_dim(stored, chan_pos * group, group, 0).astype(jnp.float32)
        updated = (
            current.astype(jnp.float32) + derivative(own) * summed.reshape(current.shape)
        ).astype(jnp.bfloat16)

        def add_kernel(total):
            values = stored.astype(jnp.float32)
            features = (
                (values * jax.nn.sigmoid(values)).astype(jnp.bfloat16).reshape(channels, cells)
            )
            return total + lax.dot_general(
                taps_mat, features, (((1,), (1,)), ((), ())), preferred_element_type=jnp.float32
            )

        def keep_kernel(total):
            return total

        kernel_sum = lax.cond(active, add_kernel, keep_kernel, kernel_sum)
        written = lax.dynamic_update_slice_in_dim(results, updated, first, 1)
        results = jnp.where(active, written, results)
        later = jnp.where(active, framed, later)
        if tick + 1 < ticks:
            inbound = shifted(updated, "section", 1)
    kernel_total = lax.psum(kernel_sum.astype(jnp.bfloat16), "frame")
    return (results[None], kernel_total.reshape(1, 27, group, channels))


def solution(mesh):
    placed = (
        P("chan", None, "frame", None),
        P("section", None, None, "frame", None),
        P("section", None, "chan", None),
    )
    return jax.shard_map(
        body,
        mesh=mesh,
        in_specs=placed,
        out_specs=(P("section", "chan", None, "frame", None), P("section", None, "chan", None)),
        check_vma=False,
    )
```

profile of v0, /device:TPU:6, one launch (start us, length us, event | category | flops | bytes accessed | tf_op | source)
XLA Modules:
  0.0 595.2 jit_solution(7948391413461682318)
XLA Ops:
  8.2 4.3 collective-permute-start
  14.0 4.6 collective-permute-done.1
  23.6 43.7 %reduce-scatter.8.cloned.1.call-done = bf16[64,256]{1,0:T(8,128)(2,1)} async-done(((bf16[512,256]{1,0:T(8,128)(2,1)}), bf16[64,256]{1,0:T(8,128)(2,1)}) %reduce-scatter.8.cloned.1.call-update) | async-done | bytes 32784 | tf_op jit(solution)/shard_map/reduce_scatter | solution.py:93
  69.7 4.5 collective-permute-done.2
  74.3 3.5 collective-permute-start.3
  79.4 4.2 collective-permute-done.4
  88.8 38.9 %reduce-scatter.10.cloned.1.call-done = bf16[64,256]{1,0:T(8,128)(2,1)} async-done(((bf16[512,256]{1,0:T(8,128)(2,1)}), bf16[64,256]{1,0:T(8,128)(2,1)}) %reduce-scatter.10.cloned.1.call-update) | async-done | bytes 32784 | tf_op jit(solution)/shard_map/reduce_scatter | solution.py:93
  130.1 4.5 collective-permute-done.5
  134.6 3.6 collective-permute-start.6
  139.8 4.2 collective-permute-done.7
  148.9 40.5 %reduce-scatter.12.cloned.1.call-done = bf16[64,256]{1,0:T(8,128)(2,1)} async-done(((bf16[512,256]{1,0:T(8,128)(2,1)}), bf16[64,256]{1,0:T(8,128)(2,1)}) %reduce-scatter.12.cloned.1.call-update) | async-done | bytes 32784 | tf_op jit(solution)/shard_map/reduce_scatter | solution.py:93
  191.7 4.5 collective-permute-done.8
  197.6 4.7 collective-permute-start.9
  208.1 2.4 conditional.17
  208.1 2.4 fusion.224
  211.3 39.8 %reduce-scatter.14.cloned.1.call-done = bf16[64,256]{1,0:T(8,128)(2,1)} async-done(((bf16[512,256]{1,0:T(8,128)(2,1)}), bf16[64,256]{1,0:T(8,128)(2,1)}) %reduce-scatter.14.cloned.1.call-update) | async-done | bytes 32784 | tf_op jit(solution)/shard_map/reduce_scatter | solution.py:93
  253.5 4.5 collective-permute-done.11
  258.0 3.6 collective-permute-start.12
  263.2 4.2 collective-permute-done.13
  271.4 2.4 conditional.18
  271.4 2.4 fusion.225
  274.6 38.1 %reduce-scatter.16.cloned.1.call-done = bf16[64,256]{1,0:T(8,128)(2,1)} async-done(((bf16[512,256]{1,0:T(8,128)(2,1)}), bf16[64,256]{1,0:T(8,128)(2,1)}) %reduce-scatter.16.cloned.1.call-update) | async-done | bytes 32784 | tf_op jit(solution)/shard_map/reduce_scatter | solution.py:93
  315.0 4.5 collective-permute-done.14
  319.6 3.7 collective-permute-start.15
  324.9 4.2 collective-permute-done.16
  333.5 2.4 conditional.19
  333.5 2.4 fusion.226
  336.7 38.0 %reduce-scatter.18.cloned.1.call-done = bf16[64,256]{1,0:T(8,128)(2,1)} async-done(((bf16[512,256]{1,0:T(8,128)(2,1)}), bf16[64,256]{1,0:T(8,128)(2,1)}) %reduce-scatter.18.cloned.1.call-update) | async-done | bytes 32784 | tf_op jit(solution)/shard_map/reduce_scatter | solution.py:93
  377.0 4.5 collective-permute-done.17
  381.6 3.7 collective-permute-start.18
  386.8 4.2 collective-permute-done.19
  395.1 2.4 conditional.20
  395.1 2.4 fusion.227
  399.2 6.4 %conditional.24 = (f32[1728,512]{1,0:T(8,128)S(1)}) conditional(s32[]{:T(128)} %convert_element_type.281, f32[1728,512]{1,0:T(8,128)S(1)} %get-tuple-element.298, (bf16[1,512,8,1,128]{4,2,3,1,0:T(8,128)(2,1)}, bf16[1728,256]{1,0:T(8,128)(2,1)}, f32[1728,512]{1,0:T(8,128)S(1)}, s32[]{:T(128)}) %tuple.127), branch_computations={%region_27.28_spmd, %region_28.29_spmd.clone} | conditional | flops 454656000 | bytes 11894796 | solution.py:116
  399.2 3.4 copy.30
  403.7 1.9 bitcast_add_fusion.2
  405.6 6.6 %conditional.25 = (f32[1728,512]{1,0:T(8,128)S(1)}) conditional(s32[]{:T(128)} %convert_element_type.287, f32[1728,512]{1,0:T(8,128)S(1)} %get-tuple-element.299, (bf16[1,512,8,1,128]{4,2,3,1,0:T(8,128)(2,1)}, bf16[1728,256]{1,0:T(8,128)(2,1)}, f32[1728,512]{1,0:T(8,128)S(1)}, s32[]{:T(128)}) %tuple.128), branch_computations={%region_29.30_spmd, %region_30.31_spmd.clone} | conditional | flops 454656000 | bytes 11894796 | solution.py:116
  405.8 3.4 copy.31
  410.3 1.9 bitcast_add_fusion.3
  412.2 6.4 %conditional.26 = (f32[1728,512]{1,0:T(8,128)S(1)}) conditional(s32[]{:T(128)} %convert_element_type.293, f32[1728,512]{1,0:T(8,128)S(1)} %get-tuple-element.300, (bf16[1,512,8,1,128]{4,2,3,1,0:T(8,128)(2,1)}, bf16[1728,256]{1,0:T(8,128)(2,1)}, f32[1728,512]{1,0:T(8,128)S(1)}, s32[]{:T(128)}) %tuple.129), branch_computations={%region_31.32_spmd, %region_32.33_spmd.clone} | conditional | flops 454656000 | bytes 11894796 | solution.py:116
  412.2 3.4 copy.32
  416.7 1.9 bitcast_add_fusion.4
  418.6 7.5 %conditional.27 = (f32[1728,512]{1,0:T(8,128)S(1)}) conditional(s32[]{:T(128)} %convert_element_type.299, f32[1728,512]{1,0:T(8,128)S(1)} %get-tuple-element.301, (bf16[1,512,8,1,128]{4,2,3,1,0:T(8,128)(2,1)}, s32[]{:T(128)}, bf16[1728,256]{1,0:T(8,128)(2,1)}, f32[1728,512]{1,0:T(8,128)S(1)}) %tuple.115), branch_computations={%region_33.34_spmd, %region_34.35_spmd} | conditional | flops 454656000 | bytes 11370508 | solution.py:116
  418.8 3.4 copy.26
  423.9 2.2 bitcast_add_fusion.5
  428.5 7.6 %reduce-scatter.20.cloned.1.call-done = bf16[64,256]{1,0:T(8,128)(2,1)} async-done(((bf16[512,256]{1,0:T(8,128)(2,1)}), bf16[64,256]{1,0:T(8,128)(2,1)}) %reduce-scatter.20.cloned.1.call-update) | async-done | bytes 32784 | tf_op jit(solution)/shard_map/reduce_scatter | solution.py:93
  438.1 147.2 %all-reduce.10.cloned.1.call-done = bf16[1,27,64,512]{3,2,1,0:T(8,128)(2,1)} async-done(((bf16[1,27,64,512]{3,2,1,0:T(8,128)(2,1)}), bf16[1,27,64,512]{3,2,1,0:T(8,128)(2,1)}) %all-reduce.10.cloned.1.call-update) | async-done | bytes 1769488 | tf_op jit(solution)/shard_map/psum | solution.py:122
  585.2 2.9 copy.307
  (311 shorter events, 72.5 us)
Async XLA Ops:
  7.2 60.2 %reduce-scatter.8.cloned.1.call-start = ((), (), s32[]{:S(2)}) async-start(), calls=%async_computation.7 | async-start | bytes 294912 | tf_op jit(solution)/shard_map/reduce_scatter | solution.py:93
  8.2 5.9 collective-permute-start
  12.5 6.2 %collective-permute-start.1 = (bf16[64,2,1,128]{3,1,0,2:T(2,128)(2,1)S(1)}, bf16[64,2,1,128]{3,1,0,2:T(2,128)(2,1)S(1)}, u32[]{:S(2)}, u32[]{:S(2)}) collective-permute-start(bf16[64,2,1,128]{3,1,0,2:T(2,128)(2,1)S(1)} %broadcast_select_fusion.18), channel_id=1, source_target_pairs={{8,0},{16,8},{24,16},{32,24},{40,32},{48,40},{56,48},{64,56},{72,6... | collective-permute-start | bytes 98312 | tf_op jit(solution)/shard_map/ppermute | solution.py:19
  22.7 45.4 %copy-start = (bf16[1,512,8,1,128]{4,2,3,1,0:T(8,128)(2,1)S(1)}, bf16[1,512,8,1,128]{4,2,3,1,0:T(8,128)(2,1)}, u32[]{:S(2)}) copy-start(bf16[1,512,8,1,128]{4,2,3,1,0:T(8,128)(2,1)} %param.32) | copy-start | bytes 3145732
  22.7 45.4 %copy-start.10 = (bf16[64,8,1,128]{3,1,2,0:T(8,128)(2,1)S(1)}, bf16[64,8,1,128]{3,1,2,0:T(8,128)(2,1)}, u32[]{:S(2)}) copy-start(bf16[64,8,1,128]{3,1,2,0:T(8,128)(2,1)} %param.31) | copy-start | bytes 393220
  22.8 0.7 copy-start.3
  23.5 104.2 %reduce-scatter.10.cloned.1.call-start = ((), (), s32[]{:S(2)}) async-start(), calls=%async_computation.8 | async-start | bytes 294912 | tf_op jit(solution)/shard_map/reduce_scatter | solution.py:93
  68.4 5.8 collective-permute-start.2
  74.3 5.1 collective-permute-start.3
  77.8 5.8 collective-permute-start.4
  88.0 0.7 copy-start.4
  88.7 100.7 %reduce-scatter.12.cloned.1.call-start = ((), (), s32[]{:S(2)}) async-start(), calls=%async_computation.9 | async-start | bytes 294912 | tf_op jit(solution)/shard_map/reduce_scatter | solution.py:93
  128.7 5.8 collective-permute-start.5
  134.6 5.1 collective-permute-start.6
  138.2 5.8 collective-permute-start.7
  148.1 0.7 copy-start.5
  148.8 102.3 %reduce-scatter.14.cloned.1.call-start = ((), (), s32[]{:S(2)}) async-start(), calls=%async_computation.10 | async-start | bytes 294912 | tf_op jit(solution)/shard_map/reduce_scatter | solution.py:93
  190.4 5.8 collective-permute-start.8
  196.3 6.0 %collective-permute-start.10 = (bf16[64,2,1,128]{3,1,0,2:T(2,128)(2,1)S(1)}, bf16[64,2,1,128]{3,1,0,2:T(2,128)(2,1)S(1)}, u32[]{:S(2)}, u32[]{:S(2)}) collective-permute-start(bf16[64,2,1,128]{3,1,0,2:T(2,128)(2,1)S(1)} %broadcast_select_fusion.15), channel_id=1, source_target_pairs={{8,0},{16,8},{24,16},{32,24},{40,32},{48,40},{56,48},{64,56},{72,6... | collective-permute-start | bytes 98312 | tf_op jit(solution)/shard_map/ppermute | solution.py:19
  197.6 6.1 %collective-permute-start.9 = (bf16[64,2,1,128]{3,1,0,2:T(2,128)(2,1)S(1)}, bf16[64,2,1,128]{3,1,0,2:T(2,128)(2,1)S(1)}, u32[]{:S(2)}, u32[]{:S(2)}) collective-permute-start(bf16[64,2,1,128]{3,1,0,2:T(2,128)(2,1)S(1)} %broadcast_select_fusion.15), channel_id=1, source_target_pairs={{0,8},{8,16},{16,24},{24,32},{32,40},{40,48},{48,56},{56,64},{64,7... | collective-permute-start | bytes 98312 | tf_op jit(solution)/shard_map/ppermute | solution.py:17
  210.5 0.7 copy-start.6
  211.3 101.4 %reduce-scatter.16.cloned.1.call-start = ((), (), s32[]{:S(2)}) async-start(), calls=%async_computation.11 | async-start | bytes 294912 | tf_op jit(solution)/shard_map/reduce_scatter | solution.py:93
  252.2 5.8 collective-permute-start.11
  258.0 5.1 collective-permute-start.12
  261.6 5.8 collective-permute-start.13
  273.8 0.7 copy-start.7
  274.6 100.1 %reduce-scatter.18.cloned.1.call-start = ((), (), s32[]{:S(2)}) async-start(), calls=%async_computation.12 | async-start | bytes 294912 | tf_op jit(solution)/shard_map/reduce_scatter | solution.py:93
  313.7 5.8 collective-permute-start.14
  319.6 5.3 collective-permute-start.15
  323.3 5.8 collective-permute-start.16
  335.9 0.7 copy-start.8
  336.6 99.4 %reduce-scatter.20.cloned.1.call-start = ((), (), s32[]{:S(2)}) async-start(), calls=%async_computation.13 | async-start | bytes 294912 | tf_op jit(solution)/shard_map/reduce_scatter | solution.py:93
  375.7 22.6 %copy-start.2 = (bf16[64,8,1,128]{3,1,0,2:T(8,128)(2,1)}, bf16[64,8,1,128]{3,1,0,2:T(8,128)(2,1)S(1)}, u32[]{:S(2)}) copy-start(bf16[64,8,1,128]{3,1,0,2:T(8,128)(2,1)S(1)} %get-tuple-element.271) | copy-start | bytes 393220
  375.7 5.8 collective-permute-start.17
  381.6 12.0 %copy-start.11 = (bf16[64,2,1,128]{3,1,0,2:T(2,128)(2,1)}, bf16[64,2,1,128]{3,1,0,2:T(2,128)(2,1)S(1)}, u32[]{:S(2)}) copy-start(bf16[64,2,1,128]{3,1,0,2:T(2,128)(2,1)S(1)} %broadcast_select_fusion.12) | copy-start | bytes 98308
  381.6 5.2 collective-permute-start.18
  385.3 5.8 collective-permute-start.19
  397.5 0.7 copy-start.9
  398.2 187.0 %all-reduce.10.cloned.1.call-start = ((), (), s32[]{:S(2)}) async-start(), calls=%async_computation.14 | async-start | bytes 3538944 | tf_op jit(solution)/shard_map/psum | solution.py:122
  427.5 9.3 %copy-start.12 = (bf16[64,2,1,128]{3,1,0,2:T(2,128)(2,1)S(1)}, bf16[64,2,1,128]{3,1,0,2:T(2,128)(2,1)}, u32[]{:S(2)}) copy-start(bf16[64,2,1,128]{3,1,0,2:T(2,128)(2,1)} %copy-done.11) | copy-start | bytes 98308
  438.0 150.0 %copy-start.13 = (bf16[1,64,8,1,128]{4,2,3,1,0:T(8,128)(2,1)}, bf16[1,64,8,1,128]{4,2,3,1,0:T(8,128)(2,1)S(1)}, u32[]{:S(2)}) copy-start(bf16[1,64,8,1,128]{4,2,3,1,0:T(8,128)(2,1)S(1)} %fusion.88) | copy-start | bytes 393220
Sparse Core Ops, SparseCore 0:
  23.7 43.6 reduce-scatter.7
  88.8 38.8 reduce-scatter.9
  149.0 40.3 reduce-scatter.11
  211.4 39.7 reduce-scatter.13
  274.7 37.9 reduce-scatter.15
  336.7 37.9 reduce-scatter.17
  398.3 37.6 reduce-scatter.19
  439.9 145.2 all-reduce.9
where the time goes:
time: 605 us; the launch traced here: 595 us
  waiting for transfers between devices  450 us (74%)
  local copies, waits for them, and re-layouts  54 us (9%)
  starting transfers between devices  44.3 us (7%)
  matrix products  17.4 us (3%)
  between operations  15.3 us (3%)
  other arithmetic  13.7 us (2%)
    reduce_scatter x7, waiting for transfers between devices, body(): lax.psum_scatter(lax.cond(active, busy, resting, 0).astype(jnp.bfloat16),...  247 us
    psum x1, waiting for transfers between devices, body(): kernel_total = lax.psum(kernel_sum.astype(jnp.bfloat16), 'frame')  147 us
    unnamed x216, local copies, waits for them, and re-layouts  33.3 us
    ppermute x6, waiting for transfers between devices, shifted(): lax.ppermute(value, axis, [(source, source + steps) for source in range(l...  27 us
    ppermute x7, starting transfers between devices, with_halo(): lax.ppermute(tail, axis, [(i, (i + 1) % count) for i in range(ends)])  27 us
    ppermute x7, waiting for transfers between devices, with_halo(): lax.ppermute(head, axis, [((i + 1) % count, i) for i in range(ends)])  25.7 us
    another operation x7, local copies, waits for them, and re-layouts  13.6 us
  transfers between devices with their start and end apart: 28, of which 27 were waited for; matrix products, arithmetic and copies ran while one was open for 5% of the time, Pallas kernels for 0%

commit v1 on v0

v1 whole, which is shorter than its diff:
```python
import functools

import jax
import jax.numpy as jnp
from jax import lax
from jax.experimental import pallas as pl
from jax.experimental.pallas import tpu as pltpu
from jax.sharding import PartitionSpec as P

MESH = pl.DeviceIdType.MESH
BLOCK = 2
GROUP = 64
SLAB = 9 * GROUP
DEPTH = 27 * GROUP
PADDED = 28 * GROUP


def remote(src, dst, send_sem, recv_sem, device):
    return pltpu.make_async_remote_copy(
        src_ref=src, dst_ref=dst, send_sem=send_sem, recv_sem=recv_sem, device_id=device, device_id_type=MESH
    )


def pipeline_kernel(
    sections, rows, chips, frames,
    up_ref, acts_ref, w_ref, grads_ref, wg_ref,
    g_own, g_par, x_own, x_par, wt, wp, part, recv, a32, slope, feat, acc, o32, gout,
    u_send, g_send, g_recv, f_send, f_recv, r_send, r_recv, w_send, w_recv,
):
    channels = w_ref.shape[1]
    chans = 2 * chips
    blocks = frames // BLOCK
    width = 128
    s = lax.axis_index("section")
    f = lax.axis_index("frame")
    d = lax.axis_index("chan")
    chip = d // 2
    core = d % 2
    partner = d + 1 - 2 * core

    barrier = pltpu.get_barrier_semaphore()
    peers = []
    for ds in (1, sections - 1):
        for df in (0, 1, rows - 1):
            peers.append(((s + ds) % sections, (f + df) % rows, d))
    for df in (1, rows - 1):
        peers.append((s, (f + df) % rows, d))
    peers.append((s, f, partner))
    for dq in range(1, chips):
        peers.append((s, f, ((chip + dq) % chips) * 2 + core))
    for peer in peers:
        pl.semaphore_signal(barrier, inc=1, device_id=peer, device_id_type=MESH)

    has_up = f > 0
    has_down = f < rows - 1

    for g in (g_own, g_par):
        for row in range(3):
            g[row, frames:] = jnp.zeros((2, GROUP, width), jnp.bfloat16)

        @pl.when(jnp.logical_not(has_down))
        def _():
            g[0, :frames] = jnp.zeros((frames, GROUP, width), jnp.bfloat16)

        @pl.when(jnp.logical_not(has_up))
        def _():
            g[2, :frames] = jnp.zeros((frames, GROUP, width), jnp.bfloat16)

    for x in (x_own, x_par):
        x[frames * SLAB :] = jnp.zeros((x.shape[0] - frames * SLAB, width), jnp.bfloat16)

    @pl.when(s == 0)
    def _():
        o32[...] = up_ref[...].astype(jnp.float32)
        for t in range(frames):
            g_own[1, t] = o32[pl.ds(t, GROUP, stride=frames), :].astype(jnp.bfloat16)

    for q in range(chans):
        wt[q, :, DEPTH:] = jnp.zeros((GROUP, PADDED - DEPTH), jnp.bfloat16)
    step = 2 * GROUP
    for k in range(0, DEPTH, step):
        size = min(step, DEPTH - k)
        turned = w_ref[k : k + size, :].astype(jnp.float32).T.astype(jnp.bfloat16)
        for q in range(chans):
            wt[q, :, k : k + size] = turned[q * GROUP : (q + 1) * GROUP]

    pl.semaphore_wait(barrier, len(peers))

    def frames_of(b):
        return (blocks - 1 - b) * BLOCK

    def weight_copy(q):
        return remote(wt.at[2 * q + 1 - core], wp.at[q], w_send.at[q], w_recv.at[q], (s, f, partner))

    def row_copy(src, b, slot, section, row, out_sem=g_send):
        first = frames_of(b)
        return remote(
            src,
            g_own.at[slot, pl.ds(first, BLOCK)],
            out_sem.at[b, slot],
            g_recv.at[b, slot],
            (section, row, d),
        )

    def spread(src, b, section, centre, go):
        out_sem = g_send if centre else u_send
        if centre:
            go(row_copy(src, b, 1, section, f, out_sem))

        @pl.when(has_down)
        def _():
            go(row_copy(src, b, 2, section, (f + 1) % rows, out_sem))

        @pl.when(has_up)
        def _():
            go(row_copy(src, b, 0, section, (f + rows - 1) % rows, out_sem))

    def begin(copy):
        copy.start()

    def sent(copy):
        copy.wait_send()

    def arrived(copy):
        copy.wait_recv()

    def block_of(g, b):
        return g.at[1, pl.ds(frames_of(b), BLOCK)]

    for q in range(chips):
        weight_copy(q).start()

    @pl.when(s == 0)
    def _():
        for b in range(blocks):
            spread(block_of(g_own, b), b, s, False, begin)

    def forward_copy(b, slot):
        first = pl.ds(frames_of(b), BLOCK)
        return remote(
            g_own.at[slot, first], g_par.at[slot, first], f_send.at[b, slot], f_recv.at[b, slot], (s, f, partner)
        )

    def per_slot(fn):
        fn(1)
        pl.when(has_down)(lambda: fn(0))
        pl.when(has_up)(lambda: fn(2))

    def take(b):
        def one(slot):
            copy = row_copy(block_of(g_own, b), b, slot, s, f)
            if slot == 1:
                pl.when(s > 0)(lambda: copy.wait_recv())
            else:
                copy.wait_recv()
            forward_copy(b, slot).start()

        per_slot(one)

    lane = lax.broadcasted_iota(jnp.int32, (GROUP, width), 1)

    def build(g, x, t):
        for slot in range(3):
            row = g[slot, t].astype(jnp.float32)
            after = jnp.where(lane == width - 1, 0.0, pltpu.roll(row, width - 1, 1))
            before = jnp.where(lane == 0, 0.0, pltpu.roll(row, 1, 1))
            base = t * SLAB + slot * 3 * GROUP
            x[base : base + GROUP] = after.astype(jnp.bfloat16)
            x[base + GROUP : base + 2 * GROUP] = row.astype(jnp.bfloat16)
            x[base + 2 * GROUP : base + 3 * GROUP] = before.astype(jnp.bfloat16)

    def columns(x, b):
        first = frames_of(b)
        return jnp.concatenate(
            [x[t * SLAB : t * SLAB + PADDED] for t in range(first, first + BLOCK)], axis=1
        )

    def term_copy(b, q):
        return remote(
            part.at[b, q], recv.at[b, chip], r_send.at[b, q], r_recv.at[b, chip], (s, f, 2 * q + core)
        )

    def term_arrival(b, q):
        return remote(
            part.at[b, q], recv.at[b, q], r_send.at[b, q], r_recv.at[b, q], (s, f, 2 * q + core)
        )

    hops = sorted(range(1, chips), key=lambda o: -min(o, chips - o))

    for b in range(blocks):
        first = frames_of(b)
        take(b)
        for t in range(first, first + BLOCK):
            build(g_own, x_own, t)
        lhs = jnp.concatenate([wt[2 * q + core] for q in range(chips)], axis=0)
        total = jnp.dot(lhs, columns(x_own, b), preferred_element_type=jnp.float32)
        if b == 0:
            for q in range(chips):
                weight_copy(q).wait_recv()
        per_slot(lambda slot: forward_copy(b, slot).wait_recv())
        for t in range(first, first + BLOCK):
            build(g_par, x_par, t)
        lhs = jnp.concatenate([wp[q] for q in range(chips)], axis=0)
        total = total + jnp.dot(lhs, columns(x_par, b), preferred_element_type=jnp.float32)
        for q in range(chips):
            part[b, q] = total[q * GROUP : (q + 1) * GROUP].astype(jnp.bfloat16)
        for o in hops:
            term_copy(b, (chip + o) % chips).start()

        if b == 0:
            a32[...] = acts_ref[...].astype(jnp.float32)
            for t in range(frames):
                own = a32[pl.ds(d * (GROUP * frames) + t, GROUP, stride=frames), :]
                logistic = 1.0 / (1.0 + jnp.exp(-own))
                slope[t] = logistic * (1.0 + own * (1.0 - logistic))
                for q in range(0, channels, step):
                    values = a32[pl.ds(q * frames + t, step, stride=frames), :]
                    values = values / (1.0 + jnp.exp(-values))
                    feat[t * width : (t + 1) * width, q : q + step] = values.T.astype(jnp.bfloat16)

        cells = slice(first * width, (first + BLOCK) * width)
        for k in range(3):
            lhs = jnp.concatenate(
                [x_own[(t + k) * SLAB : (t + k + 1) * SLAB] for t in range(first, first + BLOCK)], axis=1
            )
            add = jnp.dot(lhs, feat[cells, :], preferred_element_type=jnp.float32)
            at = slice(k * SLAB, (k + 1) * SLAB)
            if b > 0:
                add = add + acc[at]
            if b == blocks - 1:
                wg_ref[at] = add.astype(jnp.bfloat16)
            else:
                acc[at] = add

        back = part[b, chip].astype(jnp.float32)
        for o in reversed(hops):
            q = (chip + o) % chips
            term_arrival(b, q).wait_recv()
            back = back + recv[b, q].astype(jnp.float32)
        for n, t in enumerate(range(first, first + BLOCK)):
            new = g_own[1, t].astype(jnp.float32) + slope[t] * back[:, n * width : (n + 1) * width]
            new = new.astype(jnp.bfloat16)
            gout[t] = new
            o32[pl.ds(t, GROUP, stride=frames), :] = new.astype(jnp.float32)

        @pl.when(s < sections - 1)
        def _():
            spread(gout.at[pl.ds(first, BLOCK)], b, (s + 1) % sections, True, begin)

    grads_ref[...] = o32[...].astype(jnp.bfloat16)

    for q in range(chips):
        weight_copy(q).wait_send()

    @pl.when(s == 0)
    def _():
        for b in range(blocks):
            spread(block_of(g_own, b), b, s, False, sent)

    for b in range(blocks):
        per_slot(lambda slot: forward_copy(b, slot).wait_send())
        for o in hops:
            term_copy(b, (chip + o) % chips).wait_send()

    pl.when(s < sections - 1)(
        lambda: [
            spread(gout.at[pl.ds(frames_of(b), BLOCK)], b, (s + 1) % sections, True, sent) for b in range(blocks)
        ] and None
    )


def pipeline(sections, rows, chips, frames, upstream, acts, weights):
    channels = weights.shape[1]
    width = 128
    blocks = frames // BLOCK
    bf16, f32 = jnp.bfloat16, jnp.float32
    dma = pltpu.SemaphoreType.DMA
    vmem = pl.BlockSpec(memory_space=pltpu.VMEM)
    depth = (frames + 2) * SLAB + GROUP
    return pl.pallas_call(
        functools.partial(pipeline_kernel, sections, rows, chips, frames),
        out_shape=(
            jax.ShapeDtypeStruct((GROUP * frames, width), bf16),
            jax.ShapeDtypeStruct((DEPTH, channels), bf16),
        ),
        in_specs=[vmem] * 3,
        out_specs=(vmem, vmem),
        scratch_shapes=[
            pltpu.VMEM((3, frames + 2, GROUP, width), bf16),
            pltpu.VMEM((3, frames + 2, GROUP, width), bf16),
            pltpu.VMEM((depth, width), bf16),
            pltpu.VMEM((depth, width), bf16),
            pltpu.VMEM((2 * chips, GROUP, PADDED), bf16),
            pltpu.VMEM((chips, GROUP, PADDED), bf16),
            pltpu.VMEM((blocks, chips, GROUP, BLOCK * width), bf16),
            pltpu.VMEM((blocks, chips, GROUP, BLOCK * width), bf16),
            pltpu.VMEM((channels * frames, width), f32),
            pltpu.VMEM((frames, GROUP, width), f32),
            pltpu.VMEM((frames * width, channels), bf16),
            pltpu.VMEM((DEPTH, channels), f32),
            pltpu.VMEM((GROUP * frames, width), f32),
            pltpu.VMEM((frames, GROUP, width), bf16),
            dma((blocks, 3)),
            dma((blocks, 3)),
            dma((blocks, 3)),
            dma((blocks, 3)),
            dma((blocks, 3)),
            dma((blocks, chips)),
            dma((blocks, chips)),
            dma((chips,)),
            dma((chips,)),
        ],
        compiler_params=pltpu.CompilerParams(collective_id=0, has_side_effects=True),
        name="pipeline",
    )(upstream, acts, weights)


def solution(mesh):
    sections, rows, chans = (mesh.shape[a] for a in ("section", "frame", "chan"))

    def body(upstream, acts, weights):
        group, frames, _, width = upstream.shape
        channels = acts.shape[1]
        grads, kernel_sum = pipeline(
            sections,
            rows,
            chans // 2,
            frames,
            upstream.reshape(group * frames, width),
            acts.reshape(channels * frames, width),
            weights.reshape(27 * group, channels),
        )
        kernel_total = lax.psum(kernel_sum, "frame")
        return grads.reshape(1, group, frames, 1, width), kernel_total.reshape(1, 27, group, channels)

    return jax.shard_map(
        body,
        mesh=mesh,
        in_specs=(
            P("chan", None, "frame", None),
            P("section", None, None, "frame", None),
            P("section", None, "chan", None),
        ),
        out_specs=(P("section", "chan", None, "frame", None), P("section", None, "chan", None)),
        check_vma=False,
    )
```

time: 605 us -> 248 us (0.41); the launches traced: 595 us -> 248 us
  waiting for transfers between devices: 450 us -> 147 us
  Pallas kernels: 0 us -> 83.5 us
  local copies, waits for them, and re-layouts: 54 us -> 3.53 us
  starting transfers between devices: 44.3 us -> 0.04 us
  matrix products: 17.4 us -> 0 us
  other arithmetic: 13.7 us -> 0 us
    reduce_scatter x7 -> x0, waiting for transfers between devices: 247 us -> none  [body(): lax.psum_scatter(lax.cond(active, busy, resting, 0).astype(jnp.bfloat16),...]
    pallas_call x0 -> x1, Pallas kernels: none -> 83.5 us  [pipeline(): pl.pallas_call(functools.partial(pipeline_kernel, sections, rows, chips,...]
    ppermute x20 -> x0, waiting for transfers between devices: 55.5 us -> none  [the longest x6 27 us: shifted(): lax.ppermute(value, axis, [(source, source + steps) for source in range(l...]
    ppermute x20 -> x0, starting transfers between devices: 44 us -> none  [the longest x7 27 us: with_halo(): lax.ppermute(tail, axis, [(i, (i + 1) % count) for i in range(ends)])]
    unnamed x216 -> x4, local copies, waits for them, and re-layouts: 33.3 us -> 3.53 us
    dot_general x8 -> x0, matrix products: 17.4 us -> none  [the longest x4 9.56 us: busy(): lax.dot_general(kernel_mat, taps_mat, (((0,), (0,)), ((), ())), preferred...]
    another operation x14 -> x0, local copies, waits for them, and re-layouts: 14.6 us -> none
    convert_element_type x8 -> x0, other arithmetic: 6.47 us -> none  [the longest x4 3.39 us: add_kernel(): values = stored.astype(jnp.float32)]
  transfers between devices with their start and end apart: 28 -> 1, of which waited for: 27 -> 1; matrix products, arithmetic and copies ran while one was open for 5% -> 0% of each run, Pallas kernels for 0% -> 0%
where the time goes in v1:
time: 248 us
  waiting for transfers between devices  147 us (59%)
  Pallas kernels  83.5 us (34%)
  between operations  14 us (6%)
  local copies, waits for them, and re-layouts  3.53 us (1%)
    psum x1, waiting for transfers between devices, body(): kernel_total = lax.psum(kernel_sum, 'frame')  147 us
    pallas_call x1, Pallas kernels, pipeline(): pl.pallas_call(functools.partial(pipeline_kernel, sections, rows, chips,...  83.5 us
  transfers between devices with their start and end apart: 1, of which 1 were waited for; matrix products, arithmetic and copies ran while one was open for 0% of the time, Pallas kernels for 0%

profile of v1, /device:TPU:6, one launch (start us, length us, event | category | flops | bytes accessed | tf_op | source)
XLA Modules:
  0.0 247.7 jit_solution(10349603301308861581)
XLA Ops:
  7.2 0.0 all-reduce.2.cloned.1.call-start
  7.2 83.5 %pipeline.1 = (bf16[512,128]{1,0:T(8,128)(2,1)}, bf16[1728,512]{1,0:T(8,128)(2,1)}) custom-call(bf16[512,128]{1,0:T(8,128)(2,1)} %bitcast.10, bf16[4096,128]{1,0:T(8,128)(2,1)} %bitcast.9, bf16[1728,512]{1,0:T(8,128)(2,1)} %bitcast.8), custom_call_target="tpu_custom_call" | custom-call | tf_op jit(solution)/shard_map/pipeline/pallas_call | solution.py:280
  90.7 0.0 copy-start
  90.7 0.0 all-reduce.2.cloned.1.call-update
  90.7 146.6 %all-reduce.2.cloned.1.call-done = bf16[1,27,64,512]{3,2,1,0:T(8,128)(2,1)} async-done(((bf16[1,27,64,512]{3,2,1,0:T(8,128)(2,1)}), bf16[1,27,64,512]{3,2,1,0:T(8,128)(2,1)}) %all-reduce.2.cloned.1.call-update) | async-done | bytes 1769488 | tf_op jit(solution)/shard_map/psum | solution.py:333
  237.4 0.0 copy-done
  237.4 0.7 copy.9
  238.0 2.9 %copy.10 = bf16[1,27,64,512]{3,2,1,0:T(8,128)(2,1)} copy(bf16[1,27,64,512]{3,2,1,0:T(8,128)(2,1)} %all-reduce.2.cloned.1.call-done) | data formatting | bytes 3538944
Async XLA Ops:
  7.2 230.2 %all-reduce.2.cloned.1.call-start = ((), (), s32[]{:S(2)}) async-start(), calls=%async_computation | async-start | bytes 3538944 | tf_op jit(solution)/shard_map/psum | solution.py:333
  90.7 146.7 %copy-start = (bf16[512,128]{1,0:T(8,128)(2,1)S(1)}, bf16[512,128]{1,0:T(8,128)(2,1)}, u32[]{:S(2)}) copy-start(bf16[512,128]{1,0:T(8,128)(2,1)} %get-tuple-element.4) | copy-start | bytes 393220
Sparse Core Ops, SparseCore 0:
  90.8 146.4 all-reduce.1

commit v2 on v1

--- a/solution.py
+++ b/solution.py
@@ -25,7 +25,9 @@
     sections, rows, chips, frames,
     up_ref, acts_ref, w_ref, grads_ref, wg_ref,
     g_own, g_par, x_own, x_par, wt, wp, part, recv, a32, slope, feat, acc, o32, gout,
+    wsum, wfin, chain, short_chain, half_sum, half_in, whole_in,
     u_send, g_send, g_recv, f_send, f_recv, r_send, r_recv, w_send, w_recv,
+    c_send, c_recv, y_send, y_recv, a_send, a_recv, b_send, b_recv, e_send, e_recv,
 ):
     channels = w_ref.shape[1]
     chans = 2 * chips
@@ -48,6 +50,15 @@
     peers.append((s, f, partner))
     for dq in range(1, chips):
         peers.append((s, f, ((chip + dq) % chips) * 2 + core))
+    ring = rows // 2
+    lanes = ring // 2
+    reach = ring // 2
+    h = f // ring
+    z = f % ring
+    across = (s, (1 - h) * ring + z, d)
+    peers.append(across)
+    for dz in (1, ring - 1):
+        peers.append((s, h * ring + (z + dz) % ring, d))
     for peer in peers:
         pl.semaphore_signal(barrier, inc=1, device_id=peer, device_id_type=MESH)
 
@@ -184,6 +195,206 @@
         return remote(
             part.at[b, q], recv.at[b, q], r_send.at[b, q], r_recv.at[b, q], (s, f, 2 * q + core)
         )
+
+    ways = (1, -1)
+    splits = (pl.ds(0, 5), pl.ds(5, 4))
+
+    def along(way):
+        return (s, h * ring + (z + way + ring) % ring, d)
+
+    def place(offset):
+        return (z + offset + 2 * ring) % ring
+
+    def piece(ref, first, count, half, owner):
+        columns = pl.ds(pl.multiple_of((owner % lanes) * width, width), width)
+        return ref.at[pl.ds(first, count), half, owner // lanes, :, columns]
+
+    def chain_copy(p, e, k):
+        if k == 0:
+            src = piece(wsum, 9 * p, 9, e, place(ways[e] * reach))
+            dst = chain.at[p, e, 0, e]
+        else:
+            src, dst = chain.at[p, e, k - 1], chain.at[p, e, k]
+        return remote(src, dst, c_send.at[p, e, k], c_recv.at[p, e, k], along(ways[e]))
+
+    def own_term(p, half, offset):
+        return piece(wsum, 9 * p, 9, half, place(offset))[...].astype(jnp.float32)
+
+    def chain_step(p, k):
+        for e, way in enumerate(ways):
+            chain_copy(p, e, k - 1).wait_recv()
+            for half in range(2):
+                term = own_term(p, half, way * (reach - k))
+                if k > 1 or half == e:
+                    term = term + chain[p, e, k - 1, half].astype(jnp.float32)
+                chain[p, e, k - 1, half] = term.astype(jnp.bfloat16)
+            chain_copy(p, e, k).start()
+
+    def half_copy(p):
+        return remote(half_sum.at[p, 1 - h], half_in.at[p], y_send.at[p], y_recv.at[p], across)
+
+    def chain_end(p):
+        for e in range(2):
+            chain_copy(p, e, reach - 1).wait_recv()
+        for half in range(2):
+            term = own_term(p, half, 0)
+            for e in range(2):
+                term = term + chain[p, e, reach - 1, half].astype(jnp.float32)
+            half_sum[p, half] = term.astype(jnp.bfloat16)
+        half_copy(p).start()
+
+    def share_copy(p, half):
+        at = piece(wfin, 9 * p, 9, half, z)
+        return remote(at, at, b_send.at[p], b_recv.at[p], across)
+
+    def gather_copy(p, e, k, half, arrival=False):
+        at = piece(wfin, 9 * p, 9, half, place(-ways[e] * (k + 1 if arrival else k)))
+        return remote(at, at, a_send.at[p, e, k, half], a_recv.at[p, e, k, half], along(ways[e]))
+
+    def half_end(p):
+        half_copy(p).wait_recv()
+        final = half_sum[p, h].astype(jnp.float32) + half_in[p].astype(jnp.float32)
+        piece(wfin, 9 * p, 9, h, z)[...] = final.astype(jnp.bfloat16)
+        share_copy(p, h).start()
+        for e in range(2):
+            gather_copy(p, e, 0, h).start()
+
+    def share_end(p):
+        share_copy(p, 1 - h).wait_recv()
+        for e in range(2):
+            gather_copy(p, e, 0, 1 - h).start()
+
+    def gather_step(p, k):
+        for half in (h, 1 - h):
+            for e in range(2):
+                gather_copy(p, e, k - 1, half, True).wait_recv()
+                if k < reach - 1:
+                    gather_copy(p, e, k, half).start()
+        if k == reach - 1:
+            for e in range(2):
+                gather_copy(p, e, k, e).start()
+
+    def gather_end(p):
+        for e in range(2):
+            gather_copy(p, e, reach - 1, e, True).wait_recv()
+
+    def whole_copy():
+        return remote(wsum.at[pl.ds(0, 9), 1 - h], whole_in, y_send.at[0], y_recv.at[0], across)
+
+    def short_copy(e, k):
+        if k == 0:
+            taps = splits[e]
+            src = piece(wsum, taps.start, taps.size, h, place(ways[e] * reach))
+            dst = short_chain.at[e, 0, taps]
+        else:
+            src, dst = short_chain.at[e, k - 1], short_chain.at[e, k]
+        return remote(src, dst, c_send.at[0, e, k], c_recv.at[0, e, k], along(ways[e]))
+
+    def whole_end():
+        whole_copy().wait_recv()
+        for n in range(9):
+            both = wsum[n, h].astype(jnp.float32) + whole_in[n].astype(jnp.float32)
+            wsum[n, h] = both.astype(jnp.bfloat16)
+        for e in range(2):
+            short_copy(e, 0).start()
+
+    def short_step(k):
+        for e, way in enumerate(ways):
+            short_copy(e, k - 1).wait_recv()
+            for n in range(9):
+                term = piece(wsum, n, 1, h, place(way * (reach - k)))[...].astype(jnp.float32)
+                low = splits[e].start
+                if k > 1 or low <= n < low + splits[e].size:
+                    term = term + short_chain[e, k - 1, n].astype(jnp.float32)
+                short_chain[e, k - 1, n] = term[0].astype(jnp.bfloat16)
+            short_copy(e, k).start()
+
+    def cross_copy(n, owner, half):
+        at = piece(wfin, 0, 9, half, owner)
+        return remote(at, at, e_send.at[n], e_recv.at[n], across)
+
+    def spread_copy(e, k, arrival=False):
+        owner = place(-ways[e] * (k + 1 if arrival else k))
+        first, count = (splits[e].start, splits[e].size) if k == reach - 1 else (0, 9)
+        at = piece(wfin, first, count, h, owner)
+        return remote(at, at, a_send.at[0, e, k, 0], a_recv.at[0, e, k, 0], along(ways[e]))
+
+    def short_end():
+        final = own_term(0, h, 0)
+        for e in range(2):
+            short_copy(e, reach - 1).wait_recv()
+            final = final + short_chain[e, reach - 1].astype(jnp.float32)
+        piece(wfin, 0, 9, h, z)[...] = final.astype(jnp.bfloat16)
+        for e in range(2):
+            spread_copy(e, 0).start()
+        cross_copy(0, z, h).start()
+
+    def spread_step(k):
+        for e in range(2):
+            spread_copy(e, k - 1, True).wait_recv()
+            spread_copy(e, k).start()
+            cross_copy(1 + 2 * (k - 1) + e, place(-ways[e] * k), h).start()
+
+    def spread_end():
+        for e in range(2):
+            spread_copy(e, reach - 1, True).wait_recv()
+        cross_copy(ring - 1, place(reach), h).start()
+
+    def cross_all(half, go):
+        go(cross_copy(0, z, half))
+        for k in range(1, reach):
+            for e in range(2):
+                go(cross_copy(1 + 2 * (k - 1) + e, place(-ways[e] * k), half))
+        go(cross_copy(ring - 1, place(reach), half))
+
+    later = (2, 1)
+
+    def sum_begin():
+        whole_copy().start()
+        for p in later:
+            for e in range(2):
+                chain_copy(p, e, 0).start()
+
+    def sum_finish():
+        for k in range(1, reach):
+            for p in later:
+                chain_step(p, k)
+            if k == max(1, reach - 2):
+                whole_end()
+        short_step(1)
+        for p in later:
+            chain_end(p)
+        for k in range(2, reach):
+            short_step(k)
+        for p in later:
+            half_end(p)
+        short_end()
+        for p in later:
+            share_end(p)
+        for k in range(1, reach):
+            spread_step(k)
+            for p in later:
+                gather_step(p, k)
+        spread_end()
+        for p in later:
+            gather_end(p)
+        cross_all(1 - h, arrived)
+
+    def sum_sent():
+        whole_copy().wait_send()
+        for e in range(2):
+            for k in range(reach):
+                short_copy(e, k).wait_send()
+                spread_copy(e, k).wait_send()
+        cross_all(h, sent)
+        for p in later:
+            half_copy(p).wait_send()
+            share_copy(p, h).wait_send()
+            for e in range(2):
+                for k in range(reach):
+                    chain_copy(p, e, k).wait_send()
+                    for half in range(2) if k < reach - 1 else (e,):
+                        gather_copy(p, e, k, half).wait_send()
 
     hops = sorted(range(1, chips), key=lambda o: -min(o, chips - o))
 
@@ -228,9 +439,12 @@
             if b > 0:
                 add = add + acc[at]
             if b == blocks - 1:
-                wg_ref[at] = add.astype(jnp.bfloat16)
+                wsum[9 * k : 9 * k + 9] = add.astype(jnp.bfloat16).reshape(9, 2, 2, 16, channels)
             else:
                 acc[at] = add
+
+        if b == blocks - 1:
+            sum_begin()
 
         back = part[b, chip].astype(jnp.float32)
         for o in reversed(hops):
@@ -248,6 +462,9 @@
             spread(gout.at[pl.ds(first, BLOCK)], b, (s + 1) % sections, True, begin)
 
     grads_ref[...] = o32[...].astype(jnp.bfloat16)
+    sum_finish()
+    wg_ref[...] = wfin[...]
+    sum_sent()
 
     for q in range(chips):
         weight_copy(q).wait_send()
@@ -277,11 +494,12 @@
     dma = pltpu.SemaphoreType.DMA
     vmem = pl.BlockSpec(memory_space=pltpu.VMEM)
     depth = (frames + 2) * SLAB + GROUP
+    reach = rows // 4
     return pl.pallas_call(
         functools.partial(pipeline_kernel, sections, rows, chips, frames),
         out_shape=(
             jax.ShapeDtypeStruct((GROUP * frames, width), bf16),
-            jax.ShapeDtypeStruct((DEPTH, channels), bf16),
+            jax.ShapeDtypeStruct((27, 2, 2, 16, channels), bf16),
         ),
         in_specs=[vmem] * 3,
         out_specs=(vmem, vmem),
@@ -300,6 +518,13 @@
             pltpu.VMEM((DEPTH, channels), f32),
             pltpu.VMEM((GROUP * frames, width), f32),
             pltpu.VMEM((frames, GROUP, width), bf16),
+            pltpu.VMEM((27, 2, 2, 16, channels), bf16),
+            pltpu.VMEM((27, 2, 2, 16, channels), bf16),
+            pltpu.VMEM((3, 2, reach, 2, 9, 16, width), bf16),
+            pltpu.VMEM((2, reach, 9, 16, width), bf16),
+            pltpu.VMEM((3, 2, 9, 16, width), bf16),
+            pltpu.VMEM((3, 9, 16, width), bf16),
+            pltpu.VMEM((9, 2, 16, channels), bf16),
             dma((blocks, 3)),
             dma((blocks, 3)),
             dma((blocks, 3)),
@@ -309,6 +534,16 @@
             dma((blocks, chips)),
             dma((chips,)),
             dma((chips,)),
+            dma((3, 2, reach)),
+            dma((3, 2, reach)),
+            dma((3,)),
+            dma((3,)),
+            dma((3, 2, reach, 2)),
+            dma((3, 2, reach, 2)),
+            dma((3,)),
+            dma((3,)),
+            dma((rows // 2,)),
+            dma((rows // 2,)),
         ],
         compiler_params=pltpu.CompilerParams(collective_id=0, has_side_effects=True),
         name="pipeline",
@@ -330,8 +565,7 @@
             acts.reshape(channels * frames, width),
             weights.reshape(27 * group, channels),
         )
-        kernel_total = lax.psum(kernel_sum, "frame")
-        return grads.reshape(1, group, frames, 1, width), kernel_total.reshape(1, 27, group, channels)
+        return grads.reshape(1, group, frames, 1, width), kernel_sum.reshape(1, 27, group, channels)
 
     return jax.shard_map(
         body,

time: 248 us -> 141 us (0.57)
  waiting for transfers between devices: 147 us -> 0 us
  Pallas kernels: 83.5 us -> 136 us
  between operations: 14 us -> 0.64 us
    psum x1 -> x0, waiting for transfers between devices: 147 us -> none  [body(): kernel_total = lax.psum(kernel_sum, 'frame')]
    pallas_call x1, Pallas kernels: 83.5 us -> 136 us  [pipeline(): pl.pallas_call(functools.partial(pipeline_kernel, sections, rows, chips,...]
  transfers between devices with their start and end apart: 1 -> 0, of which waited for: 1 -> 0; matrix products, arithmetic and copies ran while one was open for 0% -> 0% of each run, Pallas kernels for 0% -> 0%
where the time goes in v2:
time: 141 us
  Pallas kernels  136 us (96%)
  local copies, waits for them, and re-layouts  4.44 us (3%)
    pallas_call x1, Pallas kernels, pipeline(): pl.pallas_call(functools.partial(pipeline_kernel, sections, rows, chips,...  136 us
    unnamed x2, local copies, waits for them, and re-layouts  4.44 us

profile of v2, /device:TPU:6, one launch (start us, length us, event | category | flops | bytes accessed | tf_op | source)
XLA Modules:
  0.0 140.7 jit_solution(288780615608499657)
XLA Ops:
  0.6 135.7 %pipeline.1 = (bf16[512,128]{1,0:T(8,128)(2,1)}, bf16[27,2,2,16,512]{4,3,2,1,0:T(8,128)(2,1)}) custom-call(bf16[512,128]{1,0:T(8,128)(2,1)} %bitcast.10, bf16[4096,128]{1,0:T(8,128)(2,1)} %bitcast.9, bf16[1728,512]{1,0:T(8,128)(2,1)} %bitcast.8), custom_call_target="tpu_custom_call" | custom-call | tf_op jit(solution)/shard_map/pipeline/pallas_call | solution.py:498
  136.3 1.6 %copy.8 = bf16[1,64,8,1,128]{4,2,3,1,0:T(8,128)(2,1)} copy(bf16[1,64,8,1,128]{4,2,3,1,0:T(8,128)(2,1)} %bitcast.11) | data formatting | bytes 262144
  137.9 2.9 %copy.9 = bf16[1,27,64,512]{3,2,1,0:T(8,128)(2,1)} copy(bf16[1,27,64,512]{3,2,1,0:T(8,128)(2,1)} %bitcast.7) | data formatting | bytes 3538944

commit v3 on v2

--- a/solution.py
+++ b/solution.py
@@ -8,7 +8,9 @@
 from jax.sharding import PartitionSpec as P
 
 MESH = pl.DeviceIdType.MESH
-BLOCK = 2
+CUTS = (2, 2, 2, 2)
+AHEAD = 2
+CROSS = 2
 GROUP = 64
 SLAB = 9 * GROUP
 DEPTH = 27 * GROUP
@@ -25,13 +27,13 @@
     sections, rows, chips, frames,
     up_ref, acts_ref, w_ref, grads_ref, wg_ref,
     g_own, g_par, x_own, x_par, wt, wp, part, recv, a32, slope, feat, acc, o32, gout,
-    wsum, wfin, chain, short_chain, half_sum, half_in, whole_in,
+    wsum, wfin, chain, short_chain, last_in, half_in, whole_in, g16,
     u_send, g_send, g_recv, f_send, f_recv, r_send, r_recv, w_send, w_recv,
-    c_send, c_recv, y_send, y_recv, a_send, a_recv, b_send, b_recv, e_send, e_recv,
+    c_send, c_recv, y_send, y_recv, a_send, a_recv, b_send, b_recv, e_send, e_recv, l_send, l_recv, o_sem,
 ):
     channels = w_ref.shape[1]
     chans = 2 * chips
-    blocks = frames // BLOCK
+    blocks = len(CUTS)
     width = 128
     s = lax.axis_index("section")
     f = lax.axis_index("frame")
@@ -58,7 +60,8 @@
     across = (s, (1 - h) * ring + z, d)
     peers.append(across)
     for dz in (1, ring - 1):
-        peers.append((s, h * ring + (z + dz) % ring, d))
+        for row in (h, 1 - h):
+            peers.append((s, row * ring + (z + dz) % ring, d))
     for peer in peers:
         pl.semaphore_signal(barrier, inc=1, device_id=peer, device_id_type=MESH)
 
@@ -98,7 +101,10 @@
     pl.semaphore_wait(barrier, len(peers))
 
     def frames_of(b):
-        return (blocks - 1 - b) * BLOCK
+        return frames - sum(CUTS[: b + 1])
+
+    def range_of(b):
+        return range(frames_of(b), frames_of(b) + CUTS[b])
 
     def weight_copy(q):
         return remote(wt.at[2 * q + 1 - core], wp.at[q], w_send.at[q], w_recv.at[q], (s, f, partner))
@@ -107,7 +113,7 @@
         first = frames_of(b)
         return remote(
             src,
-            g_own.at[slot, pl.ds(first, BLOCK)],
+            g_own.at[slot, pl.ds(first, CUTS[b])],
             out_sem.at[b, slot],
             g_recv.at[b, slot],
             (section, row, d),
@@ -136,7 +142,7 @@
         copy.wait_recv()
 
     def block_of(g, b):
-        return g.at[1, pl.ds(frames_of(b), BLOCK)]
+        return g.at[1, pl.ds(frames_of(b), CUTS[b])]
 
     for q in range(chips):
         weight_copy(q).start()
@@ -147,7 +153,7 @@
             spread(block_of(g_own, b), b, s, False, begin)
 
     def forward_copy(b, slot):
-        first = pl.ds(frames_of(b), BLOCK)
+        first = pl.ds(frames_of(b), CUTS[b])
         return remote(
             g_own.at[slot, first], g_par.at[slot, first], f_send.at[b, slot], f_recv.at[b, slot], (s, f, partner)
         )
@@ -181,26 +187,24 @@
             x[base + 2 * GROUP : base + 3 * GROUP] = before.astype(jnp.bfloat16)
 
     def columns(x, b):
-        first = frames_of(b)
-        return jnp.concatenate(
-            [x[t * SLAB : t * SLAB + PADDED] for t in range(first, first + BLOCK)], axis=1
+        return jnp.concatenate([x[t * SLAB : t * SLAB + PADDED] for t in range_of(b)], axis=1)
+
+    def term_copy(b, q):
+        at = pl.ds(frames_of(b), CUTS[b])
+        return remote(
+            part.at[at, q], recv.at[at, chip], r_send.at[b, q], r_recv.at[b, chip], (s, f, 2 * q + core)
         )
 
-    def term_copy(b, q):
-        return remote(
-            part.at[b, q], recv.at[b, chip], r_send.at[b, q], r_recv.at[b, chip], (s, f, 2 * q + core)
-        )
-
     def term_arrival(b, q):
-        return remote(
-            part.at[b, q], recv.at[b, q], r_send.at[b, q], r_recv.at[b, q], (s, f, 2 * q + core)
-        )
+        at = pl.ds(frames_of(b), CUTS[b])
+        return remote(part.at[at, q], recv.at[at, q], r_send.at[b, q], r_recv.at[b, q], (s, f, 2 * q + core))
 
     ways = (1, -1)
     splits = (pl.ds(0, 5), pl.ds(5, 4))
 
-    def along(way):
-        return (s, h * ring + (z + way + ring) % ring, d)
+    def along(way, side=0):
+        row = 1 - h if side else h
+        return (s, row * ring + (z + way + ring) % ring, d)
 
     def place(offset):
         return (z + offset + 2 * ring) % ring
@@ -228,20 +232,44 @@
                 if k > 1 or half == e:
                     term = term + chain[p, e, k - 1, half].astype(jnp.float32)
                 chain[p, e, k - 1, half] = term.astype(jnp.bfloat16)
-            chain_copy(p, e, k).start()
+            if k < reach - 1:
+                chain_copy(p, e, k).start()
+            else:
+                for side in range(2):
+                    last_copy(p, e, side).start()
+
+    def last_copy(p, e, side):
+        half = 1 - h if side else h
+        return remote(
+            chain.at[p, e, reach - 2, half],
+            last_in.at[p, e, side],
+            l_send.at[p, e, side],
+            l_recv.at[p, e, side],
+            along(ways[e], side),
+        )
 
     def half_copy(p):
-        return remote(half_sum.at[p, 1 - h], half_in.at[p], y_send.at[p], y_recv.at[p], across)
+        return remote(
+            piece(wsum, 9 * p, 9, 1 - h, z), half_in.at[p], y_send.at[p], y_recv.at[p], across
+        )
 
     def chain_end(p):
-        for e in range(2):
-            chain_copy(p, e, reach - 1).wait_recv()
-        for half in range(2):
-            term = own_term(p, half, 0)
+        half_copy(p).wait_recv()
+        total = own_term(p, h, 0) + half_in[p].astype(jnp.float32)
+        for side in range(2):
             for e in range(2):
-                term = term + chain[p, e, reach - 1, half].astype(jnp.float32)
-            half_sum[p, half] = term.astype(jnp.bfloat16)
-        half_copy(p).start()
+                last_copy(p, e, side).wait_recv()
+                total = total + last_in[p, e, side].astype(jnp.float32)
+        piece(wfin, 9 * p, 9, h, z)[...] = total.astype(jnp.bfloat16)
+        for side in range(2):
+            for e in range(2):
+                first_copy(p, e, side).start()
+        share_copy(p, h).start()
+
+    def first_copy(p, e, side):
+        at = piece(wfin, 9 * p, 9, h, z)
+        slot = 1 - h if side else h
+        return remote(at, at, a_send.at[p, e, 0, slot], a_recv.at[p, e, 0, h], along(ways[e], side))
 
     def share_copy(p, half):
         at = piece(wfin, 9 * p, 9, half, z)
@@ -250,19 +278,6 @@
     def gather_copy(p, e, k, half, arrival=False):
         at = piece(wfin, 9 * p, 9, half, place(-ways[e] * (k + 1 if arrival else k)))
         return remote(at, at, a_send.at[p, e, k, half], a_recv.at[p, e, k, half], along(ways[e]))
-
-    def half_end(p):
-        half_copy(p).wait_recv()
-        final = half_sum[p, h].astype(jnp.float32) + half_in[p].astype(jnp.float32)
-        piece(wfin, 9 * p, 9, h, z)[...] = final.astype(jnp.bfloat16)
-        share_copy(p, h).start()
-        for e in range(2):
-            gather_copy(p, e, 0, h).start()
-
-    def share_end(p):
-        share_copy(p, 1 - h).wait_recv()
-        for e in range(2):
-            gather_copy(p, e, 0, 1 - h).start()
 
     def gather_step(p, k):
         for half in (h, 1 - h):
@@ -275,26 +290,27 @@
                 gather_copy(p, e, k, e).start()
 
     def gather_end(p):
+        share_copy(p, 1 - h).wait_recv()
         for e in range(2):
             gather_copy(p, e, reach - 1, e, True).wait_recv()
 
     def whole_copy():
-        return remote(wsum.at[pl.ds(0, 9), 1 - h], whole_in, y_send.at[0], y_recv.at[0], across)
+        return remote(wsum.at[pl.ds(9 * CROSS, 9), 1 - h], whole_in, y_send.at[CROSS], y_recv.at[CROSS], across)
 
     def short_copy(e, k):
         if k == 0:
             taps = splits[e]
-            src = piece(wsum, taps.start, taps.size, h, place(ways[e] * reach))
+            src = piece(wsum, 9 * CROSS + taps.start, taps.size, h, place(ways[e] * reach))
             dst = short_chain.at[e, 0, taps]
         else:
             src, dst = short_chain.at[e, k - 1], short_chain.at[e, k]
-        return remote(src, dst, c_send.at[0, e, k], c_recv.at[0, e, k], along(ways[e]))
+        return remote(src, dst, c_send.at[CROSS, e, k], c_recv.at[CROSS, e, k], along(ways[e]))
 
     def whole_end():
         whole_copy().wait_recv()
         for n in range(9):
-            both = wsum[n, h].astype(jnp.float32) + whole_in[n].astype(jnp.float32)
-            wsum[n, h] = both.astype(jnp.bfloat16)
+            both = wsum[9 * CROSS + n, h].astype(jnp.float32) + whole_in[n].astype(jnp.float32)
+            wsum[9 * CROSS + n, h] = both.astype(jnp.bfloat16)
         for e in range(2):
             short_copy(e, 0).start()
 
@@ -302,7 +318,7 @@
         for e, way in enumerate(ways):
             short_copy(e, k - 1).wait_recv()
             for n in range(9):
-                term = piece(wsum, n, 1, h, place(way * (reach - k)))[...].astype(jnp.float32)
+                term = piece(wsum, 9 * CROSS + n, 1, h, place(way * (reach - k)))[...].astype(jnp.float32)
                 low = splits[e].start
                 if k > 1 or low <= n < low + splits[e].size:
                     term = term + short_chain[e, k - 1, n].astype(jnp.float32)
@@ -310,21 +326,21 @@
             short_copy(e, k).start()
 
     def cross_copy(n, owner, half):
-        at = piece(wfin, 0, 9, half, owner)
+        at = piece(wfin, 9 * CROSS, 9, half, owner)
         return remote(at, at, e_send.at[n], e_recv.at[n], across)
 
     def spread_copy(e, k, arrival=False):
         owner = place(-ways[e] * (k + 1 if arrival else k))
         first, count = (splits[e].start, splits[e].size) if k == reach - 1 else (0, 9)
-        at = piece(wfin, first, count, h, owner)
-        return remote(at, at, a_send.at[0, e, k, 0], a_recv.at[0, e, k, 0], along(ways[e]))
+        at = piece(wfin, 9 * CROSS + first, count, h, owner)
+        return remote(at, at, a_send.at[CROSS, e, k, 0], a_recv.at[CROSS, e, k, 0], along(ways[e]))
 
     def short_end():
-        final = own_term(0, h, 0)
+        final = own_term(CROSS, h, 0)
         for e in range(2):
             short_copy(e, reach - 1).wait_recv()
             final = final + short_chain[e, reach - 1].astype(jnp.float32)
-        piece(wfin, 0, 9, h, z)[...] = final.astype(jnp.bfloat16)
+        piece(wfin, 9 * CROSS, 9, h, z)[...] = final.astype(jnp.bfloat16)
         for e in range(2):
             spread_copy(e, 0).start()
         cross_copy(0, z, h).start()
@@ -347,38 +363,54 @@
                 go(cross_copy(1 + 2 * (k - 1) + e, place(-ways[e] * k), half))
         go(cross_copy(ring - 1, place(reach), half))
 
-    later = (2, 1)
-
-    def sum_begin():
-        whole_copy().start()
-        for p in later:
+    later = tuple(p for p in (2, 1, 0) if p != CROSS)
+
+    def sum_begin(p):
+        if p == CROSS:
+            whole_copy().start()
+        else:
             for e in range(2):
                 chain_copy(p, e, 0).start()
-
-    def sum_finish():
+            half_copy(p).start()
+
+    def sum_finish(between):
+        one, two = later
         for k in range(1, reach):
-            for p in later:
-                chain_step(p, k)
-            if k == max(1, reach - 2):
+            chain_step(one, k)
+            if k == 1:
+                between(0)
+            if k > 1:
+                short_step(k - 1)
+            chain_step(two, k)
+            if k == 1:
                 whole_end()
-        short_step(1)
-        for p in later:
-            chain_end(p)
-        for k in range(2, reach):
-            short_step(k)
-        for p in later:
-            half_end(p)
+            between(k)
+        chain_end(one)
+        short_step(reach - 1)
+        chain_end(two)
         short_end()
-        for p in later:
-            share_end(p)
         for k in range(1, reach):
+            gather_step(one, k)
             spread_step(k)
-            for p in later:
-                gather_step(p, k)
+            gather_step(two, k)
+        gather_end(one)
+        out_copy(one).start()
         spread_end()
-        for p in later:
-            gather_end(p)
+        gather_end(two)
+        out_copy(two).start()
         cross_all(1 - h, arrived)
+        out_copy(CROSS).start()
+
+    def out_copy(p):
+        taps = pl.ds(9 * p, 9)
+        return pltpu.make_async_copy(wfin.at[taps], wg_ref.at[taps], o_sem.at[p])
+
+    def grads_copy():
+        return pltpu.make_async_copy(g16, grads_ref, o_sem.at[3])
+
+    def grads_out():
+        g16[...] = o32[...].astype(jnp.bfloat16)
+        grads_copy().start()
 
     def sum_sent():
         whole_copy().wait_send()
@@ -391,80 +423,130 @@
             half_copy(p).wait_send()
             share_copy(p, h).wait_send()
             for e in range(2):
-                for k in range(reach):
+                for side in range(2):
+                    last_copy(p, e, side).wait_send()
+                    first_copy(p, e, side).wait_send()
+                for k in range(reach - 1):
                     chain_copy(p, e, k).wait_send()
+                for k in range(1, reach):
                     for half in range(2) if k < reach - 1 else (e,):
                         gather_copy(p, e, k, half).wait_send()
 
     hops = sorted(range(1, chips), key=lambda o: -min(o, chips - o))
 
-    for b in range(blocks):
-        first = frames_of(b)
-        take(b)
-        for t in range(first, first + BLOCK):
-            build(g_own, x_own, t)
+    last = sections - 1
+    final = blocks - 1
+
+    def prepare():
+        a32[...] = acts_ref[...].astype(jnp.float32)
+        for t in range(frames):
+            own = a32[pl.ds(d * (GROUP * frames) + t, GROUP, stride=frames), :]
+            logistic = 1.0 / (1.0 + jnp.exp(-own))
+            slope[t] = logistic * (1.0 + own * (1.0 - logistic))
+            for q in range(0, channels, step):
+                values = a32[pl.ds(q * frames + t, step, stride=frames), :]
+                values = values / (1.0 + jnp.exp(-values))
+                feat[t * width : (t + 1) * width, q : q + step] = values.T.astype(jnp.bfloat16)
+
+    def back_terms(b):
         lhs = jnp.concatenate([wt[2 * q + core] for q in range(chips)], axis=0)
         total = jnp.dot(lhs, columns(x_own, b), preferred_element_type=jnp.float32)
         if b == 0:
             for q in range(chips):
                 weight_copy(q).wait_recv()
         per_slot(lambda slot: forward_copy(b, slot).wait_recv())
-        for t in range(first, first + BLOCK):
+        for t in range_of(b):
             build(g_par, x_par, t)
         lhs = jnp.concatenate([wp[q] for q in range(chips)], axis=0)
         total = total + jnp.dot(lhs, columns(x_par, b), preferred_element_type=jnp.float32)
-        for q in range(chips):
-            part[b, q] = total[q * GROUP : (q + 1) * GROUP].astype(jnp.bfloat16)
+        for n, t in enumerate(range_of(b)):
+            for q in range(chips):
+                block = total[q * GROUP : (q + 1) * GROUP, n * width : (n + 1) * width]
+                part[t, q] = block.astype(jnp.bfloat16)
         for o in hops:
             term_copy(b, (chip + o) % chips).start()
 
-        if b == 0:
-            a32[...] = acts_ref[...].astype(jnp.float32)
-            for t in range(frames):
-                own = a32[pl.ds(d * (GROUP * frames) + t, GROUP, stride=frames), :]
-                logistic = 1.0 / (1.0 + jnp.exp(-own))
-                slope[t] = logistic * (1.0 + own * (1.0 - logistic))
-                for q in range(0, channels, step):
-                    values = a32[pl.ds(q * frames + t, step, stride=frames), :]
-                    values = values / (1.0 + jnp.exp(-values))
-                    feat[t * width : (t + 1) * width, q : q + step] = values.T.astype(jnp.bfloat16)
-
-        cells = slice(first * width, (first + BLOCK) * width)
+    def kernel_terms(b):
         for k in range(3):
-            lhs = jnp.concatenate(
-                [x_own[(t + k) * SLAB : (t + k + 1) * SLAB] for t in range(first, first + BLOCK)], axis=1
-            )
-            add = jnp.dot(lhs, feat[cells, :], preferred_element_type=jnp.float32)
             at = slice(k * SLAB, (k + 1) * SLAB)
-            if b > 0:
-                add = add + acc[at]
-            if b == blocks - 1:
+            source = [t for t in range_of(b) if t >= k]
+            add = None
+            if source:
+                lhs = jnp.concatenate([x_own[t * SLAB : (t + 1) * SLAB] for t in source], axis=1)
+                cells = slice((source[0] - k) * width, (source[-1] - k + 1) * width)
+                add = jnp.dot(lhs, feat[cells, :], preferred_element_type=jnp.float32)
+                if b > 0:
+                    add = add + acc[at]
+            if source and source[0] == k:
                 wsum[9 * k : 9 * k + 9] = add.astype(jnp.bfloat16).reshape(9, 2, 2, 16, channels)
-            else:
+            elif source:
                 acc[at] = add
 
-        if b == blocks - 1:
-            sum_begin()
-
-        back = part[b, chip].astype(jnp.float32)
+    def update(b):
         for o in reversed(hops):
-            q = (chip + o) % chips
-            term_arrival(b, q).wait_recv()
-            back = back + recv[b, q].astype(jnp.float32)
-        for n, t in enumerate(range(first, first + BLOCK)):
-            new = g_own[1, t].astype(jnp.float32) + slope[t] * back[:, n * width : (n + 1) * width]
-            new = new.astype(jnp.bfloat16)
+            term_arrival(b, (chip + o) % chips).wait_recv()
+        for t in range_of(b):
+            back = part[t, chip].astype(jnp.float32)
+            for o in hops:
+                back = back + recv[t, (chip + o) % chips].astype(jnp.float32)
+            new = (g_own[1, t].astype(jnp.float32) + slope[t] * back).astype(jnp.bfloat16)
             gout[t] = new
             o32[pl.ds(t, GROUP, stride=frames), :] = new.astype(jnp.float32)
-
-        @pl.when(s < sections - 1)
+        part_out = gout.at[pl.ds(frames_of(b), CUTS[b])]
+        pl.when(s < last)(lambda: spread(part_out, b, (s + 1) % sections, True, begin))
+
+    def complete(b):
+        return [k for k in (2, 1, 0) if k in range_of(b)]
+
+    pl.when(s > 0)(prepare)
+    for b in range(blocks):
+        take(b)
+        for t in range_of(b):
+            build(g_own, x_own, t)
+
+        @pl.when(s == last)
         def _():
-            spread(gout.at[pl.ds(first, BLOCK)], b, (s + 1) % sections, True, begin)
-
-    grads_ref[...] = o32[...].astype(jnp.bfloat16)
-    sum_finish()
-    wg_ref[...] = wfin[...]
+            kernel_terms(b)
+            for k in complete(b):
+                sum_begin(k)
+
+        if b < final:
+            back_terms(b)
+        else:
+            pl.when(s < last)(lambda: back_terms(final))
+        if b == 0:
+            pl.when(s == 0)(prepare)
+        if b >= AHEAD - 1:
+            if b < final:
+                update(b - AHEAD + 1)
+            else:
+                pl.when(s < last)(lambda: update(final - AHEAD + 1))
+
+    @pl.when(s < last)
+    def _():
+        for b in range(blocks - AHEAD + 1, blocks):
+            update(b)
+        grads_out()
+        for b in range(blocks):
+            kernel_terms(b)
+            for k in complete(b):
+                sum_begin(k)
+
+    def between(k):
+        @pl.when(s == last)
+        def _():
+            if k == 0:
+                back_terms(final)
+            if k == min(2, reach - 1):
+                for b in range(final - AHEAD + 1, blocks):
+                    update(b)
+                grads_out()
+
+    sum_finish(between)
     sum_sent()
+    for p in range(3):
+        out_copy(p).wait()
+    grads_copy().wait()
 
     for q in range(chips):
         weight_copy(q).wait_send()
@@ -481,7 +563,7 @@
 
     pl.when(s < sections - 1)(
         lambda: [
-            spread(gout.at[pl.ds(frames_of(b), BLOCK)], b, (s + 1) % sections, True, sent) for b in range(blocks)
+            spread(gout.at[pl.ds(frames_of(b), CUTS[b])], b, (s + 1) % sections, True, sent) for b in range(blocks)
         ] and None
     )
 
@@ -489,7 +571,7 @@
 def pipeline(sections, rows, chips, frames, upstream, acts, weights):
     channels = weights.shape[1]
     width = 128
-    blocks = frames // BLOCK
+    blocks = len(CUTS)
     bf16, f32 = jnp.bfloat16, jnp.float32
     dma = pltpu.SemaphoreType.DMA
     vmem = pl.BlockSpec(memory_space=pltpu.VMEM)
@@ -502,7 +584,7 @@
             jax.ShapeDtypeStruct((27, 2, 2, 16, channels), bf16),
         ),
         in_specs=[vmem] * 3,
-        out_specs=(vmem, vmem),
+        out_specs=(pl.BlockSpec(memory_space=pl.ANY),) * 2,
         scratch_shapes=[
             pltpu.VMEM((3, frames + 2, GROUP, width), bf16),
             pltpu.VMEM((3, frames + 2, GROUP, width), bf16),
@@ -510,8 +592,8 @@
             pltpu.VMEM((depth, width), bf16),
             pltpu.VMEM((2 * chips, GROUP, PADDED), bf16),
             pltpu.VMEM((chips, GROUP, PADDED), bf16),
-            pltpu.VMEM((blocks, chips, GROUP, BLOCK * width), bf16),
-            pltpu.VMEM((blocks, chips, GROUP, BLOCK * width), bf16),
+            pltpu.VMEM((frames, chips, GROUP, width), bf16),
+            pltpu.VMEM((frames, chips, GROUP, width), bf16),
             pltpu.VMEM((channels * frames, width), f32),
             pltpu.VMEM((frames, GROUP, width), f32),
             pltpu.VMEM((frames * width, channels), bf16),
@@ -522,9 +604,10 @@
             pltpu.VMEM((27, 2, 2, 16, channels), bf16),
             pltpu.VMEM((3, 2, reach, 2, 9, 16, width), bf16),
             pltpu.VMEM((2, reach, 9, 16, width), bf16),
-            pltpu.VMEM((3, 2, 9, 16, width), bf16),
+            pltpu.VMEM((3, 2, 2, 9, 16, width), bf16),
             pltpu.VMEM((3, 9, 16, width), bf16),
             pltpu.VMEM((9, 2, 16, channels), bf16),
+            pltpu.VMEM((GROUP * frames, width), bf16),
             dma((blocks, 3)),
             dma((blocks, 3)),
             dma((blocks, 3)),
@@ -544,10 +627,53 @@
             dma((3,)),
             dma((rows // 2,)),
             dma((rows // 2,)),
+            dma((3, 2, 2)),
+            dma((3, 2, 2)),
+            dma((4,)),
         ],
         compiler_params=pltpu.CompilerParams(collective_id=0, has_side_effects=True),
         name="pipeline",
     )(upstream, acts, weights)
+
+
+def hand_over_kernel(grads_in, wg_in, grads_ref, wg_ref, g_held, w_held, in_sem, out_sem):
+    def steps(copy):
+        for n in range(9):
+            taps = pl.ds(3 * n, 3)
+            copy(n, wg_in.at[taps], w_held.at[taps], wg_ref.at[taps])
+        copy(9, grads_in, g_held, grads_ref)
+
+    def fetch(n, source, held, target):
+        pltpu.make_async_copy(source, held, in_sem.at[n]).start()
+
+    def pass_on(n, source, held, target):
+        pltpu.make_async_copy(source, held, in_sem.at[n]).wait()
+        pltpu.make_async_copy(held, target, out_sem.at[n]).start()
+
+    def finish(n, source, held, target):
+        pltpu.make_async_copy(held, target, out_sem.at[n]).wait()
+
+    steps(fetch)
+    steps(pass_on)
+    steps(finish)
+
+
+def hand_over(grads, kernel_sum):
+    anywhere = pl.BlockSpec(memory_space=pl.ANY)
+    dma = pltpu.SemaphoreType.DMA
+    return pl.pallas_call(
+        hand_over_kernel,
+        out_shape=tuple(jax.ShapeDtypeStruct(a.shape, a.dtype) for a in (grads, kernel_sum)),
+        in_specs=[anywhere] * 2,
+        out_specs=(anywhere,) * 2,
+        scratch_shapes=[
+            pltpu.VMEM(grads.shape, grads.dtype),
+            pltpu.VMEM(kernel_sum.shape, kernel_sum.dtype),
+            dma((10,)),
+            dma((10,)),
+        ],
+        name="hand_over",
+    )(grads, kernel_sum)
 
 
 def solution(mesh):
@@ -565,6 +691,7 @@
             acts.reshape(channels * frames, width),
             weights.reshape(27 * group, channels),
         )
+        grads, kernel_sum = hand_over(grads, kernel_sum)
         return grads.reshape(1, group, frames, 1, width), kernel_sum.reshape(1, 27, group, channels)
 
     return jax.shard_map(

time: 141 us -> 113 us (0.80)
  Pallas kernels: 136 us -> 112 us
  local copies, waits for them, and re-layouts: 4.44 us -> 0 us
    pallas_call x1, Pallas kernels: 136 us -> 110 us  [pipeline(): pl.pallas_call(functools.partial(pipeline_kernel, sections, rows, chips,...]
    unnamed x2 -> x0, local copies, waits for them, and re-layouts: 4.44 us -> none
    pallas_call x0 -> x1, Pallas kernels: none -> 2.44 us  [hand_over(): pl.pallas_call(hand_over_kernel, out_shape=tuple((jax.ShapeDtypeStruct(a....]
where the time goes in v3:
time: 113 us
  Pallas kernels  112 us (99%)
    pallas_call x1, Pallas kernels, pipeline(): pl.pallas_call(functools.partial(pipeline_kernel, sections, rows, chips,...  110 us
    pallas_call x1, Pallas kernels, hand_over(): pl.pallas_call(hand_over_kernel, out_shape=tuple((jax.ShapeDtypeStruct(a....  2.44 us

profile of v3, /device:TPU:6, one launch (start us, length us, event | category | flops | bytes accessed | tf_op | source)
XLA Modules:
  0.0 113.1 jit_solution(15281673828806920863)
XLA Ops:
  0.6 110.1 %pipeline.1 = (bf16[512,128]{1,0:T(8,128)(2,1)}, bf16[27,2,2,16,512]{4,3,2,1,0:T(8,128)(2,1)}) custom-call(bf16[512,128]{1,0:T(8,128)(2,1)} %bitcast.9, bf16[4096,128]{1,0:T(8,128)(2,1)} %bitcast.8, bf16[1728,512]{1,0:T(8,128)(2,1)} %bitcast.7), custom_call_target="tpu_custom_call" | custom-call | tf_op jit(solution)/shard_map/pipeline/pallas_call | solution.py:580
  110.7 2.4 %hand_over.1 = (bf16[512,128]{1,0:T(8,128)(2,1)}, bf16[27,2,2,16,512]{4,3,2,1,0:T(8,128)(2,1)}) custom-call(bf16[512,128]{1,0:T(8,128)(2,1)} %get-tuple-element.6.grads_in, bf16[27,2,2,16,512]{4,3,2,1,0:T(8,128)(2,1)} %get-tuple-element.7.wg_in), custom_call_target="tpu_custom_call" | custom-call | tf_op jit(solution)/shard_map/hand_over/pallas_call | solution.py:664

commit v4 on v3

--- a/solution.py
+++ b/solution.py
@@ -517,10 +517,7 @@
         if b == 0:
             pl.when(s == 0)(prepare)
         if b >= AHEAD - 1:
-            if b < final:
-                update(b - AHEAD + 1)
-            else:
-                pl.when(s < last)(lambda: update(final - AHEAD + 1))
+            pl.when(s < last)(lambda: update(b - AHEAD + 1))
 
     @pl.when(s < last)
     def _():
@@ -538,7 +535,7 @@
             if k == 0:
                 back_terms(final)
             if k == min(2, reach - 1):
-                for b in range(final - AHEAD + 1, blocks):
+                for b in range(blocks):
                     update(b)
                 grads_out()
 

time: 113 us -> 113 us (level)
  no operation moved by 1% of the time
where the time goes in v4:
time: 113 us
  Pallas kernels  113 us (100%)
    pallas_call x1, Pallas kernels, pipeline(): pl.pallas_call(functools.partial(pipeline_kernel, sections, rows, chips,...  110 us
    pallas_call x1, Pallas kernels, hand_over(): pl.pallas_call(hand_over_kernel, out_shape=tuple((jax.ShapeDtypeStruct(a....  2.44 us

profile of v4, /device:TPU:6, one launch (start us, length us, event | category | flops | bytes accessed | tf_op | source)
XLA Modules:
  0.0 113.3 jit_solution(6381471557320410247)
XLA Ops:
  0.6 110.2 %pipeline.1 = (bf16[512,128]{1,0:T(8,128)(2,1)}, bf16[27,2,2,16,512]{4,3,2,1,0:T(8,128)(2,1)}) custom-call(bf16[512,128]{1,0:T(8,128)(2,1)} %bitcast.9, bf16[4096,128]{1,0:T(8,128)(2,1)} %bitcast.8, bf16[1728,512]{1,0:T(8,128)(2,1)} %bitcast.7), custom_call_target="tpu_custom_call" | custom-call | tf_op jit(solution)/shard_map/pipeline/pallas_call | solution.py:577
  110.8 2.4 %hand_over.1 = (bf16[512,128]{1,0:T(8,128)(2,1)}, bf16[27,2,2,16,512]{4,3,2,1,0:T(8,128)(2,1)}) custom-call(bf16[512,128]{1,0:T(8,128)(2,1)} %get-tuple-element.6.grads_in, bf16[27,2,2,16,512]{4,3,2,1,0:T(8,128)(2,1)} %get-tuple-element.7.wg_in), custom_call_target="tpu_custom_call" | custom-call | tf_op jit(solution)/shard_map/hand_over/pallas_call | solution.py:661

commit v5 on v3

--- a/solution.py
+++ b/solution.py
@@ -514,7 +514,7 @@
             back_terms(b)
         else:
             pl.when(s < last)(lambda: back_terms(final))
-        if b == 0:
+        if b == min(1, final):
             pl.when(s == 0)(prepare)
         if b >= AHEAD - 1:
             if b < final:

time: 113 us -> 114 us (level)
  no operation moved by 1% of the time
where the time goes in v5:
time: 114 us
  Pallas kernels  113 us (99%)
    pallas_call x1, Pallas kernels, pipeline(): pl.pallas_call(functools.partial(pipeline_kernel, sections, rows, chips,...  111 us
    pallas_call x1, Pallas kernels, hand_over(): pl.pallas_call(hand_over_kernel, out_shape=tuple((jax.ShapeDtypeStruct(a....  2.44 us

profile of v5, /device:TPU:6, one launch (start us, length us, event | category | flops | bytes accessed | tf_op | source)
XLA Modules:
  0.0 113.9 jit_solution(7886451625152220032)
XLA Ops:
  0.6 110.9 %pipeline.1 = (bf16[512,128]{1,0:T(8,128)(2,1)}, bf16[27,2,2,16,512]{4,3,2,1,0:T(8,128)(2,1)}) custom-call(bf16[512,128]{1,0:T(8,128)(2,1)} %bitcast.9, bf16[4096,128]{1,0:T(8,128)(2,1)} %bitcast.8, bf16[1728,512]{1,0:T(8,128)(2,1)} %bitcast.7), custom_call_target="tpu_custom_call" | custom-call | tf_op jit(solution)/shard_map/pipeline/pallas_call | solution.py:580
  111.5 2.4 %hand_over.1 = (bf16[512,128]{1,0:T(8,128)(2,1)}, bf16[27,2,2,16,512]{4,3,2,1,0:T(8,128)(2,1)}) custom-call(bf16[512,128]{1,0:T(8,128)(2,1)} %get-tuple-element.6.grads_in, bf16[27,2,2,16,512]{4,3,2,1,0:T(8,128)(2,1)} %get-tuple-element.7.wg_in), custom_call_target="tpu_custom_call" | custom-call | tf_op jit(solution)/shard_map/hand_over/pallas_call | solution.py:664
